TPU v7x, 256 devices: a whole 4x4x8 slice. The times are simulated.
256 devices in a mesh: replica: 4 (over x_hi, core), fsdp: 64 (over z, y, x_lo).
Axes of the slice: x: 4 (x_hi: 2, x_lo: 2; x = x_hi * 2 + x_lo), y: 4, z: 8, core: 2. Of those that a mesh axis runs over, the one named last changes fastest.
Arguments:
- deltas: bfloat16 [4, 2, 2048, 16384], P('replica', None, 'fsdp'), may hold values from -3 to 3
- master: float32 [2, 2048, 16384], P(None, 'replica', 'fsdp'), may hold values from -3 to 3
- momentum: float32 [2, 2048, 16384], P(None, 'replica', 'fsdp'), may hold values from -2 to 2
Outputs:
- master_out: float32 [2, 2048, 16384], P(None, 'replica', 'fsdp')
- momentum_out: float32 [2, 2048, 16384], P(None, 'replica', 'fsdp')
- params_out: bfloat16 [2, 2048, 16384], P(None, 'fsdp')
All inputs are finite; a program needn't handle non-finite values.
Results may differ from a plain program's by a relative error of at most 0.008.
Values may be sent and summed in bfloat16 or wider, within the bound.
No kernel may reach another device: no remote copies, remote signals or barrier semaphores. Data moves between devices by JAX's collectives and lax.ppermute only.
A program may use at most 64 MiB of HBM per device.

v0:
```python
import jax
import jax.numpy as jnp
from jax import lax
from jax.sharding import PartitionSpec as P


def split_up(value, dim, size):
    before, after = (value.shape[:dim], value.shape[dim + 1 :])
    return jnp.moveaxis(value.reshape(*before, size, -1, *after), dim, 0)


def cut_rows(length, count):
    unit = 8 if length >= 8 * count else 1
    return [length // unit * k // count * unit for k in range(1, count)]


def laid_out(blocks, dim):
    blocks = jnp.moveaxis(blocks, 0, dim)
    shape = blocks.shape
    return blocks.reshape(*shape[:dim], shape[dim] * shape[dim + 1], *shape[dim + 2 :])


def cut_exchange(value, axis, pieces, split_dim, concat_dim):
    blocks = split_up(value, split_dim, lax.axis_size(axis))
    widest = max(range(1, max(2, blocks.ndim - 1)), key=lambda d: blocks.shape[d])
    outs = []
    for slab in jnp.split(blocks, cut_rows(blocks.shape[widest], pieces), axis=widest):
        if slab.size:
            outs.append(lax.all_to_all(slab, axis, split_axis=0, concat_axis=0, tiled=True))
    return laid_out(jnp.concatenate(outs, axis=widest), concat_dim)


def summed_on_arrival(value, axis, dim):
    blocks = split_up(value, dim, lax.axis_size(axis))
    arrived = lax.all_to_all(blocks, axis, split_axis=0, concat_axis=0, tiled=True)
    return arrived.astype(jnp.float32).sum(axis=0)


def from_everyone(value, axis):
    copies = jnp.broadcast_to(value, (lax.axis_size(axis), *value.shape))
    return lax.all_to_all(copies, axis, split_axis=0, concat_axis=0, tiled=True)


def collect(value, axis, dim):
    blocks = from_everyone(value, axis)
    return laid_out(blocks, dim)


def on_device(deltas, master, momentum):
    local = deltas[0]
    groups = lax.axis_size("replica")
    moved = cut_exchange(local, "fsdp", 2, 2, 1)
    summed = summed_on_arrival(moved.astype(jnp.float32).astype(jnp.bfloat16), "replica", 1)
    outer = summed / groups
    velocity = 0.9 * momentum + outer
    updated = master - 0.7 * (outer + 0.9 * velocity)
    rounded = updated.astype(jnp.bfloat16)
    copies = collect(rounded, "replica", 1)
    spread = lax.all_to_all(copies, "fsdp", split_axis=1, concat_axis=2, tiled=True)
    return (updated, velocity, spread)


def solution(mesh):
    return jax.shard_map(
        on_device,
        mesh=mesh,
        in_specs=(
            P("replica", None, "fsdp", None),
            P(None, "replica", "fsdp"),
            P(None, "replica", "fsdp"),
        ),
        out_specs=(P(None, "replica", "fsdp"), P(None, "replica", "fsdp"), P(None, "fsdp", None)),
        check_vma=False,
    )
```

profile of v0, /device:TPU:2, one launch (start us, length us, event | category | flops | bytes accessed | tf_op | source)
XLA Modules:
  0.0 215.4 jit_solution(5978255964979203829)
XLA Ops:
  0.6 2.1 copy.19
  2.8 0.2 bitcast_bitcast_fusion
  3.0 0.1 fusion.1
  3.2 1.6 copy.8
  4.7 13.1 %all-to-all-start = ((bf16[64,2,16,256]{3,2,1,0:T(8,128)(2,1)}), bf16[64,2,16,256]{3,2,1,0:T(8,128)(2,1)S(1)}, u32[]{:S(2)}, u32[]{:S(2)}) async-start(bf16[64,2,16,256]{3,2,1,0:T(8,128)(2,1)} %copy.8), calls=%async_computation | async-start | bytes 2097152 | tf_op jit(solution)/shard_map/all_to_all | solution.py:29
  17.8 0.6 copy.9
  18.4 27.3 %all-to-all-done = bf16[64,2,16,256]{3,2,1,0:T(8,128)(2,1)S(1)} async-done(((bf16[64,2,16,256]{3,2,1,0:T(8,128)(2,1)}), bf16[64,2,16,256]{3,2,1,0:T(8,128)(2,1)S(1)}, u32[]{:S(2)}, u32[]{:S(2)}) %all-to-all-start) | async-done | bytes 1048608 | tf_op jit(solution)/shard_map/all_to_all | solution.py:29
  45.8 33.8 %all_to_all.38 = bf16[64,2,16,256]{3,2,1,0:T(8,128)(2,1)S(1)} all-to-all(bf16[64,2,16,256]{3,2,1,0:T(8,128)(2,1)S(1)} %copy.9), channel_id=1, replica_groups=mesh['replica'=4,'fsdp'=64] {'fsdp'}, dimensions={0} | all-to-all | bytes 2097152 | tf_op jit(solution)/shard_map/all_to_all | solution.py:29
  79.6 0.3 pad_maximum_fusion
  79.9 0.2 copy.17
  80.1 0.1 copy.12
  80.2 30.4 %all_to_all.39 = bf16[4,2,512,256]{3,2,1,0:T(8,128)(2,1)S(1)} all-to-all(bf16[4,2,512,256]{3,2,1,0:T(8,128)(2,1)S(1)} %copy.12), channel_id=1, replica_groups=mesh['replica'=4,'fsdp'=64] {'replica'}, dimensions={0} | all-to-all | bytes 4194304 | tf_op jit(solution)/shard_map/all_to_all | solution.py:35
  110.6 0.0 copy-start
  110.6 0.3 convert_reduce_fusion
  110.9 0.9 copy-done
  111.8 0.3 copy-done.1
  112.1 1.6 fusion
  113.7 0.1 broadcast_in_dim.3
  113.9 29.6 %all_to_all.40 = bf16[4,2,512,256]{3,2,1,0:T(8,128)(2,1)S(1)} all-to-all(bf16[4,2,512,256]{3,2,1,0:T(8,128)(2,1)S(1)} %broadcast_in_dim.3), channel_id=1, replica_groups=mesh['replica'=4,'fsdp'=64] {'replica'}, dimensions={0} | all-to-all | bytes 4194304 | tf_op jit(solution)/shard_map/all_to_all | solution.py:41
  143.5 0.1 copy.13
  143.6 12.8 %copy.14 = bf16[2,2048,256]{2,0,1:T(2,128)(2,1)S(1)} copy(bf16[2,2048,256]{2,1,0:T(8,128)(2,1)S(1)} %bitcast.23) | data formatting | bytes 4194304 | tf_op jit(solution)/shard_map/reshape | solution.py:20
  156.5 57.3 %all_to_all.41 = bf16[2,2048,256]{2,0,1:T(2,128)(2,1)S(1)} all-to-all(bf16[2,2048,256]{2,0,1:T(2,128)(2,1)S(1)} %copy.14), channel_id=1, replica_groups=mesh['replica'=4,'fsdp'=64] {'fsdp'}, dimensions={1} | all-to-all | bytes 4194304 | tf_op jit(solution)/shard_map/all_to_all | solution.py:59
  213.7 0.3 copy.15
  214.0 1.5 copy.18
  (1 shorter events, 0.0 us)
Async XLA Ops:
  4.7 41.0 %all-to-all-start = ((bf16[64,2,16,256]{3,2,1,0:T(8,128)(2,1)}), bf16[64,2,16,256]{3,2,1,0:T(8,128)(2,1)S(1)}, u32[]{:S(2)}, u32[]{:S(2)}) async-start(bf16[64,2,16,256]{3,2,1,0:T(8,128)(2,1)} %copy.8), calls=%async_computation | async-start | bytes 2097152 | tf_op jit(solution)/shard_map/all_to_all | solution.py:29
  110.6 1.2 copy-start
  110.6 1.5 copy-start.1
where the time goes:
time: 216 us; the launch traced here: 215 us
  blocking collectives  151 us (70%)
  waiting for transfers between devices  27.3 us (13%)
  local copies, waits for them, and re-layouts  21 us (10%)
  starting transfers between devices  13.1 us (6%)
  other arithmetic  2.22 us (1%)
    all_to_all x1, blocking collectives, on_device(): lax.all_to_all(copies, 'fsdp', split_axis=1, concat_axis=2, tiled=True)  57.3 us
    all_to_all x1, blocking collectives, cut_exchange(): lax.all_to_all(slab, axis, split_axis=0, concat_axis=0, tiled=True)  33.8 us
    all_to_all x1, blocking collectives, summed_on_arrival(): lax.all_to_all(blocks, axis, split_axis=0, concat_axis=0, tiled=True)  30.4 us
    all_to_all x1, blocking collectives, from_everyone(): return lax.all_to_all(copies, axis, split_axis=0, concat_axis=0, tiled=True)  29.6 us
    all_to_all x1, waiting for transfers between devices, cut_exchange(): lax.all_to_all(slab, axis, split_axis=0, concat_axis=0, tiled=True)  27.3 us
    all_to_all x1, starting transfers between devices, cut_exchange(): lax.all_to_all(slab, axis, split_axis=0, concat_axis=0, tiled=True)  13.1 us
    reshape x1, local copies, waits for them, and re-layouts, laid_out(): blocks.reshape(*shape[:dim], shape[dim] * shape[dim + 1], *shape[dim + 2:])  12.8 us
  transfers between devices with their start and end apart: 1, of which 1 were waited for; matrix products, arithmetic and copies ran while one was open for 0% of the time, Pallas kernels for 0%

commit v1 on v0

--- a/solution.py
+++ b/solution.py
@@ -56,7 +56,10 @@
     updated = master - 0.7 * (outer + 0.9 * velocity)
     rounded = updated.astype(jnp.bfloat16)
     copies = collect(rounded, "replica", 1)
-    spread = lax.all_to_all(copies, "fsdp", split_axis=1, concat_axis=2, tiled=True)
+    spread = jnp.concatenate(
+        lax.all_to_all(jnp.stack(jnp.split(copies, lax.axis_size("fsdp"), axis=1)), "fsdp", 0, 0),
+        axis=2,
+    )
     return (updated, velocity, spread)
 
 

time: 216 us -> 204 us (0.944)
  local copies, waits for them, and re-layouts: 21 us -> 8.23 us
    reshape x1, local copies, waits for them, and re-layouts: 12.8 us -> 1.45 us  [on_device(): jnp.concatenate(lax.all_to_all(jnp.stack(jnp.split(copies, lax.axis_size(...]
where the time goes in v1:
time: 204 us; the launch traced here: 203 us
  blocking collectives  151 us (74%)
  waiting for transfers between devices  27.3 us (13%)
  starting transfers between devices  13.1 us (6%)
  local copies, waits for them, and re-layouts  8.23 us (4%)
  other arithmetic  2.22 us (1%)
    all_to_all x1, blocking collectives, on_device(): lax.all_to_all(jnp.stack(jnp.split(copies, lax.axis_size('fsdp'), axis=1)...  57.3 us
    all_to_all x1, blocking collectives, cut_exchange(): lax.all_to_all(slab, axis, split_axis=0, concat_axis=0, tiled=True)  33.8 us
    all_to_all x1, blocking collectives, summed_on_arrival(): lax.all_to_all(blocks, axis, split_axis=0, concat_axis=0, tiled=True)  30.4 us
    all_to_all x1, blocking collectives, from_everyone(): return lax.all_to_all(copies, axis, split_axis=0, concat_axis=0, tiled=True)  29.6 us
    all_to_all x1, waiting for transfers between devices, cut_exchange(): lax.all_to_all(slab, axis, split_axis=0, concat_axis=0, tiled=True)  27.3 us
    all_to_all x1, starting transfers between devices, cut_exchange(): lax.all_to_all(slab, axis, split_axis=0, concat_axis=0, tiled=True)  13.1 us
  transfers between devices with their start and end apart: 1, of which 1 were waited for; matrix products, arithmetic and copies ran while one was open for 0% of the time, Pallas kernels for 0%

profile of v1, /device:TPU:2, one launch (start us, length us, event | category | flops | bytes accessed | tf_op | source)
XLA Modules:
  0.0 203.2 jit_solution(8389351432701186727)
XLA Ops:
  0.6 2.1 %copy.80 = bf16[8,8,64,256]{3,2,1,0:T(8,128)(2,1)S(1)} copy(bf16[8,8,64,256]{3,1,2,0:T(8,128)(2,1)} %bitcast.343) | data formatting | bytes 4194304
  2.8 0.2 bitcast_bitcast_fusion
  3.0 0.1 fusion.1
  3.2 1.6 copy.71
  4.7 13.1 %all-to-all-start = ((bf16[64,2,16,256]{3,2,1,0:T(8,128)(2,1)}), bf16[64,2,16,256]{3,2,1,0:T(8,128)(2,1)S(1)}, u32[]{:S(2)}, u32[]{:S(2)}) async-start(bf16[64,2,16,256]{3,2,1,0:T(8,128)(2,1)} %copy.71), calls=%async_computation | async-start | bytes 2097152 | tf_op jit(solution)/shard_map/all_to_all | solution.py:29
  17.8 0.6 copy.72
  18.4 27.3 %all-to-all-done = bf16[64,2,16,256]{3,2,1,0:T(8,128)(2,1)S(1)} async-done(((bf16[64,2,16,256]{3,2,1,0:T(8,128)(2,1)}), bf16[64,2,16,256]{3,2,1,0:T(8,128)(2,1)S(1)}, u32[]{:S(2)}, u32[]{:S(2)}) %all-to-all-start) | async-done | bytes 1048608 | tf_op jit(solution)/shard_map/all_to_all | solution.py:29
  45.8 33.8 %all_to_all.25 = bf16[64,2,16,256]{3,2,1,0:T(8,128)(2,1)S(1)} all-to-all(bf16[64,2,16,256]{3,2,1,0:T(8,128)(2,1)S(1)} %copy.72), channel_id=1, replica_groups=mesh['replica'=4,'fsdp'=64] {'fsdp'}, dimensions={0} | all-to-all | bytes 2097152 | tf_op jit(solution)/shard_map/all_to_all | solution.py:29
  79.6 0.3 pad_maximum_fusion
  79.9 0.2 copy.78
  80.1 0.1 copy.75
  80.2 30.4 %all_to_all.26 = bf16[4,2,512,256]{3,2,1,0:T(8,128)(2,1)S(1)} all-to-all(bf16[4,2,512,256]{3,2,1,0:T(8,128)(2,1)S(1)} %copy.75), channel_id=1, replica_groups=mesh['replica'=4,'fsdp'=64] {'replica'}, dimensions={0} | all-to-all | bytes 4194304 | tf_op jit(solution)/shard_map/all_to_all | solution.py:35
  110.6 0.0 copy-start
  110.6 0.0 copy-start.1
  110.6 0.3 convert_reduce_fusion
  110.9 0.9 copy-done
  111.8 0.3 copy-done.1
  112.1 1.6 fusion
  113.7 0.1 broadcast_in_dim.3
  113.9 29.6 %all_to_all.27 = bf16[4,2,512,256]{3,2,1,0:T(8,128)(2,1)S(1)} all-to-all(bf16[4,2,512,256]{3,2,1,0:T(8,128)(2,1)S(1)} %broadcast_in_dim.3), channel_id=1, replica_groups=mesh['replica'=4,'fsdp'=64] {'replica'}, dimensions={0} | all-to-all | bytes 4194304 | tf_op jit(solution)/shard_map/all_to_all | solution.py:41
  143.5 0.1 copy.76
  144.5 57.3 %all_to_all.28 = bf16[64,2,32,256]{3,2,1,0:T(8,128)(2,1)S(1)} all-to-all(bf16[64,2,32,256]{3,2,1,0:T(8,128)(2,1)S(1)} %constant_dynamic-update-slice_fusion), channel_id=1, replica_groups=mesh['replica'=4,'fsdp'=64] {'fsdp'}, dimensions={0} | all-to-all | bytes 4194304 | tf_op jit(solution)/shard_map/all_to_all | solution.py:60
  201.7 1.5 copy.79
  (64 shorter events, 0.3 us)
Async XLA Ops:
  4.7 41.0 %all-to-all-start = ((bf16[64,2,16,256]{3,2,1,0:T(8,128)(2,1)}), bf16[64,2,16,256]{3,2,1,0:T(8,128)(2,1)S(1)}, u32[]{:S(2)}, u32[]{:S(2)}) async-start(bf16[64,2,16,256]{3,2,1,0:T(8,128)(2,1)} %copy.71), calls=%async_computation | async-start | bytes 2097152 | tf_op jit(solution)/shard_map/all_to_all | solution.py:29
  110.6 1.2 copy-start
  110.6 1.5 copy-start.1
